TPU v7x, 512 devices: a whole 4x4x16 slice. The times are simulated.
512 devices in a mesh: dp: 4 (over y), ep: 128 (over z, x, core).
Axes of the slice: x: 4, y: 4, z: 16, core: 2. Of those that a mesh axis runs over, the one named last changes fastest.
Arguments:
- tokens: bfloat16 [4096, 3584], P(('dp', 'ep')), may hold values from -6 to 6
- expert_ids: int32 [4096, 8], P(('dp', 'ep')), may hold values from 0 to 127, as said below
- route_gates: float32 [4096, 8], P(('dp', 'ep')), may hold values from 0.1 to 1
- w_gate: bfloat16 [128, 3584, 1024], P('ep', None, 'dp'), may hold values from -0.09375 to 0.09375
- w_up: bfloat16 [128, 3584, 1024], P('ep', None, 'dp'), may hold values from -0.09375 to 0.09375
Outputs:
- activations: bfloat16 [4096, 8, 1024], P(('dp', 'ep'))
Inputs may be any that keep to these rules, and one draw needn't show every extreme that they name: `expert_ids`: each row names 8 different experts. Exactly 1 expert, the hot ones, are named by 8 tokens of every device each, and every token names exactly one of them. Any other expert is named by at most 2 tokens of one device, and some such expert is named by exactly 2 tokens of every device.
All inputs are finite; a program needn't handle non-finite values.
Results may differ from a plain program's by a relative error of at most 0.0049.
Values may be sent and summed in bfloat16 or wider, within the bound.
No kernel may reach another device: no remote copies, remote signals or barrier semaphores. Data moves between devices by JAX's collectives and lax.ppermute only.
A program may use at most 128 MiB of HBM per device.

v0:
```python
import jax
import jax.numpy as jnp
from jax import lax
from jax.sharding import PartitionSpec as P

HOT = 1


def from_root(value, axis, source):
    kept = jnp.where(lax.axis_index(axis) == source, value, 0).astype(value.dtype)
    return lax.psum(kept, axis)


def cold_slots(block_ids, hot_ids, experts):
    flat_ids = block_ids.reshape(-1)
    labels = jnp.arange(experts, dtype=jnp.int32)
    is_cold = jnp.logical_not(jnp.any(flat_ids[:, None] == hot_ids[None, :], axis=1))
    matches = jnp.logical_and(flat_ids[:, None] == labels[None, :], is_cold[:, None]).astype(
        jnp.int32
    )
    before = jnp.cumsum(matches, axis=0) - matches
    return (
        jnp.sum(before * matches, axis=1).reshape(block_ids.shape),
        is_cold.reshape(block_ids.shape),
    )


def selector(places_of, place_count):
    matched = places_of[None, :, :] == jnp.arange(place_count, dtype=jnp.int32)[:, None, None]
    return jnp.any(matched, axis=-1).astype(jnp.bfloat16)


def gated_hidden(row_block, gate_cols, up_cols, pattern):
    gate_part = jnp.einsum(pattern, row_block, gate_cols, preferred_element_type=jnp.float32)
    up_part = jnp.einsum(pattern, row_block, up_cols, preferred_element_type=jnp.float32)
    return (jax.nn.silu(gate_part) * up_part).astype(jnp.bfloat16)


def per_device(tokens, expert_ids, route_gates, w_gate, w_up):
    tok_rows, top_count = expert_ids.shape
    model_width = tokens.shape[1]
    local_experts = w_gate.shape[0]
    quarter = w_gate.shape[2]
    owners = lax.axis_size("ep")
    groups = lax.axis_size("dp")
    experts = owners * local_experts
    cold_experts = experts - HOT
    capacity = max(2, ((top_count - 1) * tok_rows + cold_experts - 1) // cold_experts)
    labels = jnp.arange(experts, dtype=jnp.int32)
    own_counts = jnp.sum(
        (expert_ids.reshape(-1)[:, None] == labels[None, :]).astype(jnp.int32), axis=0
    )
    scores = jnp.where(own_counts > capacity, experts - labels, 0)
    hot_ids = lax.top_k(scores, HOT)[1]
    group_tokens = lax.all_gather(tokens, "dp", axis=0, tiled=True)
    group_ids = lax.all_gather(expert_ids, "dp", axis=0, tiled=True)
    member_ids = group_ids.reshape(groups, tok_rows, top_count)
    slots, is_cold = jax.vmap(lambda block_ids: cold_slots(block_ids, hot_ids, experts))(member_ids)
    members = jnp.arange(groups, dtype=jnp.int32)[:, None, None]
    cold_place = (member_ids * groups + members) * capacity + slots
    group_place = jnp.where(is_cold, cold_place, -1).reshape(groups * tok_rows, top_count)
    places = experts * groups * capacity
    group_size = groups * tok_rows
    hot_rows = group_size // HOT
    hot_lookup = jnp.zeros((group_size, top_count), jnp.int32)
    expert = hot_ids[0]
    weight_pair = (
        lax.dynamic_index_in_dim(w_gate, expert % local_experts, 0, keepdims=False),
        lax.dynamic_index_in_dim(w_up, expert % local_experts, 0, keepdims=False),
    )
    gate_copy = from_root(weight_pair[0], "ep", expert // local_experts)
    up_copy = from_root(weight_pair[1], "ep", expert // local_experts)
    naming = jnp.any(group_ids == expert, axis=1).astype(jnp.int32)
    ranking = jnp.cumsum(naming) - naming
    chooser = jnp.logical_and(
        ranking[None, :] == jnp.arange(hot_rows, dtype=jnp.int32)[:, None], naming[None, :] > 0
    ).astype(jnp.bfloat16)
    picked_rows = jnp.dot(chooser, group_tokens, preferred_element_type=jnp.float32).astype(
        jnp.bfloat16
    )
    hot_parts = [gated_hidden(picked_rows, gate_copy, up_copy, "nd,df->nf")]
    hot_lookup = jnp.where(group_ids == expert, places + ranking[:, None], hot_lookup)
    picks = selector(group_place, places)
    outgoing = jnp.dot(picks, group_tokens, preferred_element_type=jnp.float32).astype(jnp.bfloat16)
    outgoing = outgoing.reshape(owners, local_experts, groups * capacity, model_width)
    hidden = gated_hidden(
        lax.all_to_all(outgoing, "ep", split_axis=0, concat_axis=0, tiled=True),
        w_gate,
        w_up,
        "slnd,ldf->slnf",
    )
    returned = lax.all_to_all(hidden, "ep", split_axis=0, concat_axis=0, tiled=True)
    cold_table = returned.reshape(places, quarter)
    full_table = jnp.concatenate([cold_table] + hot_parts, axis=0)
    lookup = jnp.where(group_place >= 0, group_place, hot_lookup)
    group_hidden = jnp.take(full_table, lookup.reshape(-1), axis=0).reshape(
        groups, tok_rows, top_count, quarter
    )
    home_rows = lax.all_to_all(group_hidden, "dp", split_axis=0, concat_axis=3, tiled=True)
    hidden = home_rows.reshape(tok_rows, top_count, groups * quarter)
    return (route_gates[:, :, None] * hidden.astype(jnp.float32)).astype(jnp.bfloat16)


def solution(mesh):
    return jax.shard_map(
        per_device,
        mesh=mesh,
        in_specs=(
            P(("dp", "ep"), None),
            P(("dp", "ep"), None),
            P(("dp", "ep"), None),
            P("ep", None, "dp"),
            P("ep", None, "dp"),
        ),
        out_specs=P(("dp", "ep"), None, None),
        check_vma=False,
    )
```

profile of v0, /device:TPU:1, one launch (start us, length us, event | category | flops | bytes accessed | tf_op | source)
XLA Modules:
  0.0 577.1 jit_solution(4684912742181126534)
XLA Ops:
  6.5 0.8 eq.92
  7.3 10.6 %all_gather.6 = s32[32,8]{1,0:T(8,128)S(1)} all-gather(s32[8,8]{1,0:T(8,128)} %param.6), channel_id=1, replica_groups=mesh['dp'=4,'ep'=128] {'dp'}, dimensions={0}, use_global_device_ids=true | all-gather | bytes 1280 | tf_op jit(solution)/shard_map/all_gather | solution.py:56
  18.2 2.5 top_k.11
  20.7 0.1 fusion.37
  21.3 0.1 reduce_window_sum.18
  21.5 0.3 select_reduce_fusion
  21.9 0.4 fusion.30
  22.3 9.5 %all_gather.7 = bf16[32,3584]{1,0:T(8,128)(2,1)S(1)} all-gather(bf16[8,3584]{1,0:T(8,128)(2,1)} %param.5), channel_id=1, replica_groups=mesh['dp'=4,'ep'=128] {'dp'}, dimensions={0}, use_global_device_ids=true | all-gather | bytes 286720 | tf_op jit(solution)/shard_map/all_gather | solution.py:55
  31.8 5.1 fusion.4
  37.0 25.9 %all-to-all-start = ((bf16[128,1,8,3584]{3,2,1,0:T(8,128)(2,1)}), bf16[128,1,8,3584]{3,2,1,0:T(8,128)(2,1)}, u32[]{:S(2)}, u32[]{:S(2)}) async-start(bf16[128,1,8,3584]{3,2,1,0:T(8,128)(2,1)} %fusion.4), calls=%async_computation | async-start | bytes 14680064 | tf_op jit(solution)/shard_map/all_to_all | solution.py:87
  62.8 0.2 all-reduce.3.cloned.1.call-start
  63.1 3.6 bitcast_select_fusion
  66.7 332.2 %all-to-all-done = bf16[128,1,8,3584]{3,2,1,0:T(8,128)(2,1)} async-done(((bf16[128,1,8,3584]{3,2,1,0:T(8,128)(2,1)}), bf16[128,1,8,3584]{3,2,1,0:T(8,128)(2,1)}, u32[]{:S(2)}, u32[]{:S(2)}) %all-to-all-start) | async-done | bytes 7340064 | tf_op jit(solution)/shard_map/all_to_all | solution.py:87
  398.9 7.3 %fusion.9 = f32[128,1,8,256]{3,0,2,1:T(8,128)S(1)} fusion(bf16[1,3584,256]{2,1,0:T(8,128)(2,1)S(1)} %copy-done.1, bf16[128,1,8,3584]{3,2,1,0:T(8,128)(2,1)} %all-to-all-done), kind=kOutput, calls=%fused_computation.14 | convolution fusion | flops 1879048192 | bytes 10223616 | tf_op jit(solution)/shard_map/slnd,ldf->slnf/dot_general | solution.py:34
  406.2 7.3 %fusion.24 = bf16[128,1,8,256]{3,0,2,1:T(8,128)(2,1)S(1)} fusion(bf16[1,3584,256]{2,1,0:T(8,128)(2,1)S(1)} %copy-done.2, bf16[128,1,8,3584]{3,2,1,0:T(8,128)(2,1)} %all-to-all-done, f32[128,1,8,256]{3,0,2,1:T(8,128)S(1)} %fusion.9), kind=kOutput, calls=%fused_computation.17 | convolution fusion | flops 1880621056 | bytes 10747904 | tf_op jit(solution)/shard_map/slnd,ldf->slnf/dot_general | solution.py:35
  413.5 1.1 copy.21
  414.6 13.0 %all-to-all-start.1 = ((bf16[128,1,8,256]{3,2,1,0:T(8,128)(2,1)}), bf16[128,1,8,256]{3,2,1,0:T(8,128)(2,1)S(1)}, u32[]{:S(2)}, u32[]{:S(2)}) async-start(bf16[128,1,8,256]{3,2,1,0:T(8,128)(2,1)} %copy.21), calls=%async_computation.1 | async-start | bytes 1048576 | tf_op jit(solution)/shard_map/all_to_all | solution.py:92
  427.7 0.2 convolution_convert_fusion.1
  427.9 129.1 %all-reduce.3.cloned.1.call-done = (bf16[3584,256]{1,0:T(8,128)(2,1)}, bf16[3584,256]{1,0:T(8,128)(2,1)}) async-done(((bf16[3584,256]{1,0:T(8,128)(2,1)}, bf16[3584,256]{1,0:T(8,128)(2,1)}), (bf16[3584,256]{1,0:T(8,128)(2,1)}, bf16[3584,256]{1,0:T(8,128)(2,1)})) %all-reduce.3.cloned.1.call-update) | async-done | bytes 3670032 | tf_op jit(solution)/shard_map/psum | solution.py:11
  557.0 2.0 fusion.38
  559.1 0.4 fusion.29
  559.6 1.2 gather_fusion
  560.8 8.6 %all_to_all.19 = bf16[4,8,8,256]{3,2,1,0:T(8,128)(2,1)S(1)} all-to-all(bf16[4,8,8,256]{3,2,1,0:T(8,128)(2,1)S(1)} %broadcast_select_fusion), channel_id=1, replica_groups=mesh['dp'=4,'ep'=128] {'dp'}, dimensions={0} | all-to-all | bytes 262144 | tf_op jit(solution)/shard_map/all_to_all | solution.py:99
  569.5 0.7 multiply_convert_fusion
  (32 shorter events, 1.2 us)
Async XLA Ops:
  37.0 26.2 %copy-start.1 = (bf16[1,3584,256]{2,1,0:T(8,128)(2,1)S(1)}, bf16[1,3584,256]{2,1,0:T(8,128)(2,1)}, u32[]{:S(2)}) copy-start(bf16[1,3584,256]{2,1,0:T(8,128)(2,1)} %param.8) | copy-start | bytes 5505028
  37.0 361.9 %all-to-all-start = ((bf16[128,1,8,3584]{3,2,1,0:T(8,128)(2,1)}), bf16[128,1,8,3584]{3,2,1,0:T(8,128)(2,1)}, u32[]{:S(2)}, u32[]{:S(2)}) async-start(bf16[128,1,8,3584]{3,2,1,0:T(8,128)(2,1)} %fusion.4), calls=%async_computation | async-start | bytes 14680064 | tf_op jit(solution)/shard_map/all_to_all | solution.py:87
  62.8 494.2 %all-reduce.3.cloned.1.call-start = ((), (), s32[]{:S(2)}) async-start(), calls=%async_computation.3 | async-start | bytes 7340032 | tf_op jit(solution)/shard_map/psum | solution.py:11
  398.9 7.3 %copy-start.2 = (bf16[1,3584,256]{2,1,0:T(8,128)(2,1)S(1)}, bf16[1,3584,256]{2,1,0:T(8,128)(2,1)}, u32[]{:S(2)}) copy-start(bf16[1,3584,256]{2,1,0:T(8,128)(2,1)} %param.9) | copy-start | bytes 5505028
  414.6 144.9 %all-to-all-start.1 = ((bf16[128,1,8,256]{3,2,1,0:T(8,128)(2,1)}), bf16[128,1,8,256]{3,2,1,0:T(8,128)(2,1)S(1)}, u32[]{:S(2)}, u32[]{:S(2)}) async-start(bf16[128,1,8,256]{3,2,1,0:T(8,128)(2,1)} %copy.21), calls=%async_computation.1 | async-start | bytes 1048576 | tf_op jit(solution)/shard_map/all_to_all | solution.py:92
  557.0 2.1 copy-start
  559.5 10.0 %copy-start.3 = (f32[8,8]{1,0:T(8,128)S(1)}, f32[8,8]{1,0:T(8,128)}, u32[]{:S(2)}) copy-start(f32[8,8]{1,0:T(8,128)} %param.7) | copy-start | bytes 772
Sparse Core Ops, SparseCore 0:
  67.2 489.7 all-reduce.2
where the time goes:
time: 580 us; the launch traced here: 577 us
  waiting for transfers between devices  461 us (79%)
  starting transfers between devices  39.1 us (7%)
  blocking collectives  28.7 us (5%)
  matrix products  22.4 us (4%)
  between operations  13.6 us (2%)
  other arithmetic  8.53 us (1%)
    all_to_all x1, waiting for transfers between devices, per_device(): lax.all_to_all(outgoing, 'ep', split_axis=0, concat_axis=0, tiled=True)  332 us
    psum x1, waiting for transfers between devices, from_root(): return lax.psum(kept, axis)  129 us
    all_to_all x1, starting transfers between devices, per_device(): lax.all_to_all(outgoing, 'ep', split_axis=0, concat_axis=0, tiled=True)  25.9 us
    all_to_all x1, starting transfers between devices, per_device(): lax.all_to_all(hidden, 'ep', split_axis=0, concat_axis=0, tiled=True)  13 us
  transfers between devices with their start and end apart: 3, of which 2 were waited for; matrix products, arithmetic and copies ran while one was open for 4% of the time, Pallas kernels for 0%

commit v1 on v0

v1 whole, which is shorter than its diff:
```python
import jax
import jax.numpy as jnp
from jax import lax
from jax.sharding import Mesh, PartitionSpec as P

EP_AXES = ("z", "x", "core")
ALL_AXES = ("dp",) + EP_AXES


def per_device(tokens, expert_ids, route_gates, w_gate, w_up):
    tok_rows, top_count = expert_ids.shape
    quarter = w_gate.shape[2]
    groups = lax.axis_size("dp")
    owners = lax.axis_size(EP_AXES)
    column = lax.all_gather(tokens, "z", axis=0, tiled=True)
    everyone = lax.all_gather(column, ("dp", "x", "core"), axis=0, tiled=True)
    gate_part = jnp.dot(everyone, w_gate[0], preferred_element_type=jnp.float32)
    up_part = jnp.dot(everyone, w_up[0], preferred_element_type=jnp.float32)
    hidden = (jax.nn.silu(gate_part) * up_part).astype(jnp.bfloat16)
    depth, width, cores = (lax.axis_size(a) for a in EP_AXES)
    blocks = hidden.reshape(groups, width * cores, depth, tok_rows, quarter)
    blocks = blocks.swapaxes(1, 2).reshape(groups * owners, tok_rows, quarter)
    home = lax.all_to_all(blocks, ALL_AXES, split_axis=0, concat_axis=0, tiled=True)
    table = home.reshape(groups * owners * tok_rows, quarter)
    rows = expert_ids * tok_rows + jnp.arange(tok_rows, dtype=jnp.int32)[:, None]
    starts = jnp.arange(groups, dtype=jnp.int32) * (owners * tok_rows)
    rows = starts[:, None] + rows.reshape(-1)[None, :]
    picked = jnp.take(table, rows.reshape(-1), axis=0).reshape(
        groups, tok_rows, top_count, quarter
    )
    hidden = picked.transpose(1, 2, 0, 3).reshape(tok_rows, top_count, groups * quarter)
    return (route_gates[:, :, None] * hidden.astype(jnp.float32)).astype(jnp.bfloat16)


def solution(mesh):
    depth, width, cores = 16, 4, 2
    groups = mesh.shape["dp"]
    fine = Mesh(mesh.devices.reshape(groups, depth, width, cores), ALL_AXES)
    return jax.shard_map(
        per_device,
        mesh=fine,
        in_specs=(
            P(ALL_AXES, None),
            P(ALL_AXES, None),
            P(ALL_AXES, None),
            P(EP_AXES, None, "dp"),
            P(EP_AXES, None, "dp"),
        ),
        out_specs=P(ALL_AXES, None, None),
        check_vma=False,
    )
```

time: 580 us -> 326 us (0.56)
  waiting for transfers between devices: 461 us -> 222 us
  starting transfers between devices: 39.1 us -> 20.1 us
  blocking collectives: 28.7 us -> 37.6 us
  other arithmetic: 8.53 us -> 1.02 us
    all_to_all x2 -> x1, waiting for transfers between devices: 332 us -> 100 us  [per_device(): lax.all_to_all(blocks, ALL_AXES, split_axis=0, concat_axis=0, tiled=True)]
    psum x1 -> x0, waiting for transfers between devices: 129 us -> none  [from_root(): return lax.psum(kept, axis)]
    all_gather x0 -> x1, waiting for transfers between devices: none -> 121 us  [per_device(): everyone = lax.all_gather(column, ('dp', 'x', 'core'), axis=0, tiled=True)]
    all_to_all x2 -> x1, starting transfers between devices: 38.9 us -> 20.1 us  [per_device(): lax.all_to_all(blocks, ALL_AXES, split_axis=0, concat_axis=0, tiled=True)]
    all_gather x2 -> x1, blocking collectives: 20.1 us -> 37.6 us  [per_device(): column = lax.all_gather(tokens, 'z', axis=0, tiled=True)]
    all_to_all x1 -> x0, blocking collectives: 8.63 us -> none  [per_device(): lax.all_to_all(group_hidden, 'dp', split_axis=0, concat_axis=3, tiled=True)]
    dot_general x6 -> x2, matrix products: 22.4 us -> 27.1 us  [the longest x1 13.8 us: per_device(): up_part = jnp.dot(everyone, w_up[0], preferred_element_type=jnp.float32)]
  transfers between devices with their start and end apart: 3 -> 2, of which waited for: 2 -> 2; matrix products, arithmetic and copies ran while one was open for 4% -> 0% of each run, Pallas kernels for 0% -> 0%
where the time goes in v1:
time: 326 us; the launch traced here: 325 us
  waiting for transfers between devices  222 us (68%)
  blocking collectives  37.6 us (12%)
  matrix products  27.1 us (8%)
  starting transfers between devices  20.1 us (6%)
  between operations  13.5 us (4%)
  local copies, waits for them, and re-layouts  4.62 us (1%)
    all_gather x1, waiting for transfers between devices, per_device(): everyone = lax.all_gather(column, ('dp', 'x', 'core'), axis=0, tiled=True)  121 us
    all_to_all x1, waiting for transfers between devices, per_device(): lax.all_to_all(blocks, ALL_AXES, split_axis=0, concat_axis=0, tiled=True)  100 us
    all_gather x1, blocking collectives, per_device(): column = lax.all_gather(tokens, 'z', axis=0, tiled=True)  37.6 us
    all_to_all x1, starting transfers between devices, per_device(): lax.all_to_all(blocks, ALL_AXES, split_axis=0, concat_axis=0, tiled=True)  20.1 us
    dot_general x1, matrix products, per_device(): up_part = jnp.dot(everyone, w_up[0], preferred_element_type=jnp.float32)  13.8 us
    dot_general x1, matrix products, per_device(): gate_part = jnp.dot(everyone, w_gate[0], preferred_element_type=jnp.float32)  13.3 us
  transfers between devices with their start and end apart: 2, of which 2 were waited for; matrix products, arithmetic and copies ran while one was open for 0% of the time, Pallas kernels for 0%

profile of v1, /device:TPU:1, one launch (start us, length us, event | category | flops | bytes accessed | tf_op | source)
XLA Modules:
  0.0 325.5 jit_solution(1481081159946006932)
XLA Ops:
  6.5 0.0 copy-start
  6.5 0.0 all-gather.2.cloned.1.call-start
  6.5 37.6 %all_gather.6 = bf16[128,3584]{1,0:T(8,128)(2,1)} all-gather(bf16[8,3584]{1,0:T(8,128)(2,1)} %param.5), channel_id=1, replica_groups=mesh['dp'=4,'z'=16,'x'=4,'core'=2] {'z'}, dimensions={0}, use_global_device_ids=true | all-gather | bytes 974848 | tf_op jit(solution)/shard_map/all_gather | solution.py:15
  44.1 0.0 all-gather.2.cloned.1.call-update
  44.1 121.5 %all-gather.2.cloned.1.call-done = bf16[4096,3584]{1,0:T(8,128)(2,1)} async-done(((bf16[128,3584]{1,0:T(8,128)(2,1)}), bf16[4096,3584]{1,0:T(8,128)(2,1)}) %all-gather.2.cloned.1.call-update) | async-done | bytes 29360144 | tf_op jit(solution)/shard_map/all_gather | solution.py:16
  165.6 0.0 copy-done
  165.6 0.0 copy-start.3
  165.6 13.3 %fusion.2 = f32[4096,256]{1,0:T(8,128)S(1)} fusion(bf16[4096,3584]{1,0:T(8,128)(2,1)} %all-gather.2.cloned.1.call-done, bf16[1,3584,256]{2,1,0:T(8,128)(2,1)S(1)} %copy-done), kind=kOutput, calls=%fused_computation.4 | convolution fusion | flops 7516192768 | bytes 35389440 | tf_op jit(solution)/shard_map/dot_general | solution.py:17
  178.9 0.0 copy-done.3
  179.0 13.8 %fusion = bf16[4096,256]{1,0:T(8,128)(2,1)S(1)} fusion(bf16[4096,3584]{1,0:T(8,128)(2,1)} %all-gather.2.cloned.1.call-done, f32[4096,256]{1,0:T(8,128)S(1)} %fusion.2, bf16[1,3584,256]{2,1,0:T(8,128)(2,1)S(1)} %copy-done.3), kind=kOutput, calls=%fused_computation.2 | convolution fusion | flops 7522484224 | bytes 37486592 | tf_op jit(solution)/shard_map/dot_general | solution.py:18
  192.7 0.0 copy-start.2
  192.8 1.6 copy.7
  194.3 0.0 copy-start.1
  194.3 20.1 %all-to-all-start = ((bf16[512,8,256]{2,1,0:T(8,128)(2,1)}), bf16[512,8,256]{2,1,0:T(8,128)(2,1)}, u32[]{:S(2)}, u32[]{:S(2)}) async-start(bf16[512,8,256]{2,1,0:T(8,128)(2,1)} %bitcast.18), calls=%async_computation | async-start | bytes 4194304 | tf_op jit(solution)/shard_map/all_to_all | solution.py:23
  214.5 0.0 copy-done.2
  214.5 0.1 add.78
  214.6 0.1 broadcast_add_fusion
  214.7 0.1 add.81
  214.8 0.1 fusion.6
  214.8 100.1 %all-to-all-done = bf16[512,8,256]{2,1,0:T(8,128)(2,1)} async-done(((bf16[512,8,256]{2,1,0:T(8,128)(2,1)}), bf16[512,8,256]{2,1,0:T(8,128)(2,1)}, u32[]{:S(2)}, u32[]{:S(2)}) %all-to-all-start) | async-done | bytes 2097184 | tf_op jit(solution)/shard_map/all_to_all | solution.py:23
  314.9 2.8 gather_fusion
  317.7 0.1 convert_bitcast_fusion
  317.9 0.0 copy-done.1
  317.9 0.7 multiply_convert_fusion
  (5 shorter events, 0.0 us)
Async XLA Ops:
  6.5 159.1 %copy-start = (bf16[1,3584,256]{2,1,0:T(8,128)(2,1)S(1)}, bf16[1,3584,256]{2,1,0:T(8,128)(2,1)}, u32[]{:S(2)}) copy-start(bf16[1,3584,256]{2,1,0:T(8,128)(2,1)} %param.8) | copy-start | bytes 5505028
  6.5 159.1 %all-gather.2.cloned.1.call-start = ((), (), s32[]{:S(2)}) async-start(), calls=%async_computation.1 | async-start | bytes 30277632 | tf_op jit(solution)/shard_map/all_gather | solution.py:16
  165.6 13.3 %copy-start.3 = (bf16[1,3584,256]{2,1,0:T(8,128)(2,1)S(1)}, bf16[1,3584,256]{2,1,0:T(8,128)(2,1)}, u32[]{:S(2)}) copy-start(bf16[1,3584,256]{2,1,0:T(8,128)(2,1)} %param.9) | copy-start | bytes 5505028
  192.7 21.7 %copy-start.2 = (s32[8,8]{1,0:T(8,128)S(1)}, s32[8,8]{1,0:T(8,128)}, u32[]{:S(2)}) copy-start(s32[8,8]{1,0:T(8,128)} %param.6) | copy-start | bytes 772
  194.3 123.5 %copy-start.1 = (f32[8,8]{1,0:T(8,128)S(1)}, f32[8,8]{1,0:T(8,128)}, u32[]{:S(2)}) copy-start(f32[8,8]{1,0:T(8,128)} %param.7) | copy-start | bytes 772
  194.3 120.6 %all-to-all-start = ((bf16[512,8,256]{2,1,0:T(8,128)(2,1)}), bf16[512,8,256]{2,1,0:T(8,128)(2,1)}, u32[]{:S(2)}, u32[]{:S(2)}) async-start(bf16[512,8,256]{2,1,0:T(8,128)(2,1)} %bitcast.18), calls=%async_computation | async-start | bytes 4194304 | tf_op jit(solution)/shard_map/all_to_all | solution.py:23
Sparse Core Ops, SparseCore 0:
  44.3 121.3 all-gather.1

commit v2 on v1

v2 whole, which is shorter than its diff:
```python
import functools

import jax
import jax.numpy as jnp
from jax import lax
from jax.experimental import pallas as pl
from jax.experimental.pallas import tpu as pltpu
from jax.sharding import Mesh, PartitionSpec as P

EP_AXES = ("z", "x", "core")
ALL_AXES = ("dp",) + EP_AXES
FLOW_AXES = ("dp", "x", "core", "z")
SLOTS = 2
LANES = 128
COLUMNS_PER_STEP = 4
F32 = jnp.float32
BF16 = jnp.bfloat16


def expert_kernel(own_ref, hot_ref, rows_ref, gate_ref, up_ref, cold_ref, hot_out_ref, *, tok_rows):
    width = gate_ref.shape[0]
    block = rows_ref.shape[0]
    homes = block // tok_rows
    rows = rows_ref[:, :width]
    gate_part = jnp.dot(rows, gate_ref[...], preferred_element_type=F32)
    up_part = jnp.dot(rows, up_ref[...], preferred_element_type=F32)
    hidden = (gate_part / (1.0 + jnp.exp(-gate_part)) * up_part).astype(BF16)
    wide = hidden.astype(F32)
    mine = jnp.where(hot_ref[0] > 0, wide, 0.0).astype(BF16)
    hot_out_ref[...] = mine.reshape(hot_out_ref.shape)

    ids = rows_ref[:, width:].astype(F32)
    hits = jnp.where(ids == own_ref[0].astype(F32), 1.0, 0.0).astype(BF16)
    named = jnp.dot(hits, jnp.ones((LANES, LANES), BF16), preferred_element_type=F32)
    row_at = lax.broadcasted_iota(jnp.int32, (block, block), 0)
    col_at = lax.broadcasted_iota(jnp.int32, (block, block), 1)
    earlier = jnp.logical_and(row_at // tok_rows == col_at // tok_rows, col_at < row_at)
    before = jnp.dot(
        jnp.where(earlier, 1.0, 0.0).astype(BF16), named.astype(BF16), preferred_element_type=F32
    )
    home_at = lax.broadcasted_iota(jnp.int32, (homes, block), 0)
    from_at = lax.broadcasted_iota(jnp.int32, (homes, block), 1)
    of_home = jnp.where(from_at // tok_rows == home_at, 1.0, 0.0).astype(BF16)
    quarter = hidden.shape[1]
    for slot in range(SLOTS):
        chosen = jnp.where(before == float(slot), named, 0.0)
        chosen = jnp.concatenate([chosen] * (quarter // LANES), axis=1)
        kept = (wide * chosen).astype(BF16)
        cold_ref[:, slot * quarter : (slot + 1) * quarter] = jnp.dot(
            of_home, kept, preferred_element_type=F32
        ).astype(BF16)


def home_kernel(place_ref, gate_ref, cold_ref, hot_ref, out_ref, *, groups, tok_rows):
    pairs = out_ref.shape[0]
    quarter = hot_ref.shape[2]
    owners = cold_ref.shape[0] // groups
    place = place_ref[...]
    lane_at = lax.broadcasted_iota(jnp.int32, (pairs, owners), 1)
    picks = [
        jnp.where(place == lane_at * SLOTS + slot, 1.0, 0.0).astype(BF16) for slot in range(SLOTS)
    ]
    tok_at = lax.broadcasted_iota(jnp.int32, (pairs, tok_rows), 0) // (pairs // tok_rows)
    row_at = lax.broadcasted_iota(jnp.int32, (pairs, tok_rows), 1)
    hot_pick = jnp.where(jnp.logical_and(place < 0, tok_at == row_at), 1.0, 0.0).astype(BF16)
    gates = gate_ref[...]
    for group in range(groups):
        total = jnp.dot(hot_pick, hot_ref[group], preferred_element_type=F32)
        for slot in range(SLOTS):
            total += jnp.dot(
                picks[slot],
                cold_ref[group * owners : (group + 1) * owners, slot * quarter : (slot + 1) * quarter],
                preferred_element_type=F32,
            )
        out_ref[:, group * quarter : (group + 1) * quarter] = (gates * total).astype(BF16)


def per_device(tokens, expert_ids, route_gates, w_gate, w_up):
    tok_rows, top_count = expert_ids.shape
    model_width = tokens.shape[1]
    quarter = w_gate.shape[2]
    groups = lax.axis_size("dp")
    depth, width, cores = (lax.axis_size(a) for a in EP_AXES)
    columns = width * cores
    owners = depth * columns
    total = groups * owners
    own = lax.axis_index(EP_AXES).astype(jnp.int32)

    id_part = jnp.pad(
        expert_ids.astype(BF16), ((0, 0), (0, LANES - top_count)), constant_values=-1
    )
    packed = jnp.concatenate([tokens, id_part], axis=1)
    line = lax.all_gather(packed, "z", axis=0, tiled=True)
    expert_ids, line = lax.optimization_barrier((expert_ids, line))
    everyone = lax.all_gather(line, ("dp", "x", "core"), axis=0, tiled=True)

    named_by = jnp.any(
        expert_ids[:, :, None, None] == expert_ids[None, None, :, :], axis=3
    ).astype(jnp.int32)
    is_hot = jnp.sum(named_by, axis=2) > SLOTS
    is_before = (
        jnp.arange(tok_rows)[None, None, :] < jnp.arange(tok_rows)[:, None, None]
    ).astype(jnp.int32)
    slots = jnp.sum(named_by * is_before, axis=2)
    hot_id = jnp.max(jnp.where(is_hot, expert_ids, -1))
    at_z = expert_ids // columns
    at_column = expert_ids % columns
    place = (at_column * depth + at_z) * SLOTS + slots
    place = jnp.where(is_hot, -1, place).reshape(tok_rows * top_count, 1)

    column_rows = depth * tok_rows
    per_step = COLUMNS_PER_STEP
    steps = columns // per_step
    block = per_step * column_rows
    cold, hot = pl.pallas_call(
        functools.partial(expert_kernel, tok_rows=tok_rows),
        grid=(groups * steps,),
        out_shape=(
            jax.ShapeDtypeStruct((total, SLOTS * quarter), BF16),
            jax.ShapeDtypeStruct((columns, groups, column_rows, quarter), BF16),
        ),
        in_specs=[
            pl.BlockSpec(memory_space=pltpu.SMEM),
            pl.BlockSpec(memory_space=pltpu.SMEM),
            pl.BlockSpec((block, model_width + LANES), lambda i: (i, 0)),
            pl.BlockSpec((model_width, quarter), lambda i: (0, 0)),
            pl.BlockSpec((model_width, quarter), lambda i: (0, 0)),
        ],
        out_specs=(
            pl.BlockSpec((block // tok_rows, SLOTS * quarter), lambda i: (i, 0)),
            pl.BlockSpec(
                (per_step, 1, column_rows, quarter), lambda i: (i % steps, i // steps, 0, 0)
            ),
        ),
        compiler_params=pltpu.CompilerParams(vmem_limit_bytes=48 * 2**20),
        name="expert",
    )(
        own.reshape(1),
        (own == hot_id).astype(jnp.int32).reshape(1),
        everyone,
        w_gate.reshape(model_width, quarter),
        w_up.reshape(model_width, quarter),
    )

    hot = lax.psum_scatter(
        hot.reshape(columns * groups * column_rows, quarter),
        ("x", "core"),
        scatter_dimension=0,
        tiled=True,
    )
    cold = lax.all_to_all(
        cold.reshape(total, SLOTS, quarter), FLOW_AXES, split_axis=0, concat_axis=0, tiled=True
    )
    hot = lax.all_to_all(
        hot.reshape(groups * depth, tok_rows, quarter),
        ("dp", "z"),
        split_axis=0,
        concat_axis=0,
        tiled=True,
    )
    hot = lax.dynamic_index_in_dim(
        hot.reshape(groups, depth, tok_rows, quarter), hot_id // columns, 1, keepdims=False
    )
    pairs = tok_rows * top_count
    out = pl.pallas_call(
        functools.partial(home_kernel, groups=groups, tok_rows=tok_rows),
        out_shape=jax.ShapeDtypeStruct((pairs, groups * quarter), BF16),
        name="home",
    )(place, route_gates.reshape(pairs, 1), cold.reshape(total, SLOTS * quarter), hot)
    return out.reshape(tok_rows, top_count, groups * quarter)


def solution(mesh):
    width, cores = 4, 2
    groups, depth = mesh.shape["dp"], mesh.shape["ep"] // (width * cores)
    fine = Mesh(mesh.devices.reshape(groups, depth, width, cores), ALL_AXES)
    return jax.shard_map(
        per_device,
        mesh=fine,
        in_specs=(
            P(ALL_AXES, None),
            P(ALL_AXES, None),
            P(ALL_AXES, None),
            P(EP_AXES, None, "dp"),
            P(EP_AXES, None, "dp"),
        ),
        out_specs=P(ALL_AXES, None, None),
        check_vma=False,
    )
```

time: 326 us -> 285 us (0.87)
  waiting for transfers between devices: 222 us -> 135 us
  blocking collectives: 37.6 us -> 90.8 us
  Pallas kernels: 0 us -> 27.2 us
  matrix products: 27.1 us -> 0 us
  starting transfers between devices: 20.1 us -> 4.65 us
    all_to_all x1, waiting for transfers between devices: 100 us -> 14.1 us  [per_device(): lax.all_to_all(hot.reshape(groups * depth, tok_rows, quarter), ('dp', 'z'...]
    all_to_all x0 -> x1, blocking collectives: none -> 53.4 us  [per_device(): lax.all_to_all(cold.reshape(total, SLOTS, quarter), FLOW_AXES, split_axis...]
    pallas_call x0 -> x2, Pallas kernels: none -> 27.2 us  [the longest x1 25.2 us: per_device(): pl.pallas_call(functools.partial(expert_kernel, tok_rows=tok_rows), grid=...]
    dot_general x2 -> x0, matrix products: 27.1 us -> none  [the longest x1 13.8 us: per_device(): up_part = jnp.dot(everyone, w_up[0], preferred_element_type=jnp.float32)]
    all_to_all x1, starting transfers between devices: 20.1 us -> 4.61 us  [per_device(): lax.all_to_all(hot.reshape(groups * depth, tok_rows, quarter), ('dp', 'z'...]
  transfers between devices with their start and end apart: 2 -> 3, of which waited for: 2 -> 2; matrix products, arithmetic and copies ran while one was open for 0% -> 2% of each run, Pallas kernels for 0% -> 0%
where the time goes in v2:
time: 285 us; the launch traced here: 283 us
  waiting for transfers between devices  135 us (47%)
  blocking collectives  90.8 us (32%)
  Pallas kernels  27.2 us (10%)
  between operations  16.7 us (6%)
  starting transfers between devices  4.65 us (2%)
  local copies, waits for them, and re-layouts  4.48 us (2%)
  other arithmetic  3.91 us (1%)
    all_gather x1, waiting for transfers between devices, per_device(): everyone = lax.all_gather(line, ('dp', 'x', 'core'), axis=0, tiled=True)  121 us
    all_to_all x1, blocking collectives, per_device(): lax.all_to_all(cold.reshape(total, SLOTS, quarter), FLOW_AXES, split_axis...  53.4 us
    all_gather x1, blocking collectives, per_device(): line = lax.all_gather(packed, 'z', axis=0, tiled=True)  37.4 us
    pallas_call x1, Pallas kernels, per_device(): pl.pallas_call(functools.partial(expert_kernel, tok_rows=tok_rows), grid=...  25.2 us
    all_to_all x1, waiting for transfers between devices, per_device(): lax.all_to_all(hot.reshape(groups * depth, tok_rows, quarter), ('dp', 'z'...  14.1 us
  transfers between devices with their start and end apart: 3, of which 2 were waited for; matrix products, arithmetic and copies ran while one was open for 2% of the time, Pallas kernels for 0%

profile of v2, /device:TPU:1, one launch (start us, length us, event | category | flops | bytes accessed | tf_op | source)
XLA Modules:
  0.0 283.1 jit_solution(7236844426094394586)
XLA Ops:
  6.5 0.0 all-gather.2.cloned.1.call-start
  6.5 0.8 convert_element_type.17
  7.4 0.8 fusion.1
  8.2 37.4 %all_gather.6 = bf16[128,3712]{1,0:T(8,128)(2,1)} all-gather(bf16[8,3712]{1,0:T(8,128)(2,1)S(1)} %fusion.1), channel_id=1, replica_groups=mesh['dp'=4,'z'=16,'x'=4,'core'=2] {'z'}, dimensions={0}, use_global_device_ids=true | all-gather | bytes 1009664 | tf_op jit(solution)/shard_map/all_gather | solution.py:93
  45.6 0.0 all-gather.2.cloned.1.call-update
  45.7 0.0 reduce-scatter.2.cloned.1.call-start
  45.7 0.0 copy-done.2
  45.7 1.3 compare_reduce_fusion
  47.0 0.4 select_reduce_fusion
  47.4 0.6 select_reduce_fusion.1
  48.6 121.2 %all-gather.2.cloned.1.call-done.rows_ref = bf16[4096,3712]{1,0:T(8,128)(2,1)} async-done(((bf16[128,3712]{1,0:T(8,128)(2,1)}), bf16[4096,3712]{1,0:T(8,128)(2,1)}) %all-gather.2.cloned.1.call-update) | async-done | bytes 30408720 | tf_op jit(solution)/shard_map/all_gather | solution.py:95
  169.8 0.0 copy-done
  169.8 1.5 copy-done.1
  171.3 25.2 %expert.1 = (bf16[512,512]{1,0:T(8,128)(2,1)S(1)}, bf16[8,4,128,256]{3,2,1,0:T(8,128)(2,1)}) custom-call(s32[1]{0:T(128)} %bitcast.own_ref, s32[1]{0:T(128)} %bitcast.1.hot_ref, bf16[4096,3712]{1,0:T(8,128)(2,1)} %all-gather.2.cloned.1.call-done.rows_ref, bf16[3584,256]{1,0:T(8,128)(2,1)S(1)} %bitcast.12, bf16[3584,256]{1,0:T(8,128)(2,1)S(1)} %bitcast.13), custom_call_target="tpu_custom_call" | custom-call | tf_op jit(solution)/shard_map/expert/pallas_call | solution.py:115
  196.5 0.0 reduce-scatter.2.cloned.1.call-update
  196.5 0.1 reshape.63
  196.6 53.4 %all_to_all.10 = bf16[512,2,256]{2,1,0:T(2,128)(2,1)S(1)} all-to-all(bf16[512,2,256]{2,1,0:T(2,128)(2,1)S(1)} %reshape.63), channel_id=1, replica_groups=mesh['dp'=4,'z'=16,'x'=4,'core'=2] {'dp','x','core','z'}, dimensions={0} | all-to-all | bytes 1048576 | tf_op jit(solution)/shard_map/all_to_all | solution.py:151
  250.0 4.6 %all-to-all-start.1 = ((bf16[64,8,256]{2,1,0:T(8,128)(2,1)}), bf16[64,8,256]{2,1,0:T(8,128)(2,1)S(1)}, u32[]{:S(2)}, u32[]{:S(2)}) async-start(bf16[64,8,256]{2,1,0:T(8,128)(2,1)} %bitcast.18), calls=%async_computation.2 | async-start | bytes 524288 | tf_op jit(solution)/shard_map/all_to_all | solution.py:154
  257.2 0.7 reshape.71.place_ref
  257.9 0.7 reshape.72.gate_ref
  258.6 0.9 copy.12
  259.5 14.1 %all-to-all-done.1 = bf16[64,8,256]{2,1,0:T(8,128)(2,1)S(1)} async-done(((bf16[64,8,256]{2,1,0:T(8,128)(2,1)}), bf16[64,8,256]{2,1,0:T(8,128)(2,1)S(1)}, u32[]{:S(2)}, u32[]{:S(2)}) %all-to-all-start.1) | async-done | bytes 262176 | tf_op jit(solution)/shard_map/all_to_all | solution.py:154
  273.6 0.6 dynamic-slice_bitcast_fusion.hot_ref
  274.2 2.0 home.1
  (8 shorter events, 0.0 us)
Async XLA Ops:
  6.5 39.2 %copy-start.2 = (s32[8,8]{1,0:T(8,128)S(1)}, s32[8,8]{1,0:T(8,128)}, u32[]{:S(2)}) copy-start(s32[8,8]{1,0:T(8,128)} %param.6) | copy-start | bytes 772
  6.5 163.3 %copy-start = (bf16[1,3584,256]{2,1,0:T(8,128)(2,1)S(1)}, bf16[1,3584,256]{2,1,0:T(8,128)(2,1)}, u32[]{:S(2)}) copy-start(bf16[1,3584,256]{2,1,0:T(8,128)(2,1)} %param.8) | copy-start | bytes 5505028
  6.5 163.3 %all-gather.2.cloned.1.call-start = ((), (), s32[]{:S(2)}) async-start(), calls=%async_computation.3 | async-start | bytes 31358976 | tf_op jit(solution)/shard_map/all_gather | solution.py:95
  45.7 204.3 %reduce-scatter.2.cloned.1.call-start = ((), (), s32[]{:S(2)}) async-start(), calls=%async_computation.4 | async-start | bytes 2359296 | tf_op jit(solution)/shard_map/reduce_scatter | solution.py:145
  169.8 1.5 copy-start.1
  196.5 61.4 %copy-start.3 = (f32[8,8]{1,0:T(8,128)S(1)}, f32[8,8]{1,0:T(8,128)}, u32[]{:S(2)}) copy-start(f32[8,8]{1,0:T(8,128)} %param.7) | copy-start | bytes 772
  250.0 23.6 %all-to-all-start.1 = ((bf16[64,8,256]{2,1,0:T(8,128)(2,1)}), bf16[64,8,256]{2,1,0:T(8,128)(2,1)S(1)}, u32[]{:S(2)}, u32[]{:S(2)}) async-start(bf16[64,8,256]{2,1,0:T(8,128)(2,1)} %bitcast.18), calls=%async_computation.2 | async-start | bytes 524288 | tf_op jit(solution)/shard_map/all_to_all | solution.py:154
Sparse Core Ops, SparseCore 0:
  45.8 123.9 all-gather.1
  196.6 40.3 reduce-scatter.1
